TPU v7x, 512 devices: a whole 4x8x8 slice. The times are simulated.
512 devices in a mesh: blk: 16 (over z, y_lo), tan: 32 (over y_hi, x, core).
Axes of the slice: x: 4, y: 8 (y_hi: 4, y_lo: 2; y = y_hi * 2 + y_lo), z: 8, core: 2. Of those that a mesh axis runs over, the one named last changes fastest.
Arguments:
- layer_in: bfloat16 [2048, 256], P('blk'), may hold values from -6 to 6
- laplace_in: bfloat16 [2048, 256], P('blk'), may hold values from -6 to 6
- tangent_in: bfloat16 [2048, 64, 256], P('blk', 'tan'), may hold values from -1.5 to 1.5
- spin_labels: int32 [2048], P('blk'), may hold values from 0 to 1
- pair_bias: bfloat16 [2048, 2048], P('blk'), may hold values from -6 to 306
- query_weight: bfloat16 [256, 256], replicated, may hold values from -0.375 to 0.375
- key_weight: bfloat16 [256, 256], replicated, may hold values from -0.375 to 0.375
- value_weight: bfloat16 [256, 256], replicated, may hold values from -0.375 to 0.375
- out_weight: bfloat16 [256, 256], replicated, may hold values from -0.375 to 0.375
- head_gain: float32 [4], replicated, may hold values from 0.5 to 2
- spin_gain: float32 [4], replicated, may hold values from -2 to 2
Outputs:
- layer_out: bfloat16 [2048, 256], P('blk')
- tangent_out: bfloat16 [2048, 64, 256], P('blk', 'tan')
- laplacian_out: float32 [2048, 256], P('blk')
All inputs are finite; a program needn't handle non-finite values.
Results may differ from a plain program's by a relative error of at most 0.02.
Values may be sent and summed in bfloat16 or wider, within the bound.
A program may use at most 64 MiB of HBM per device.

v0:
```python
import math
import jax
import jax.numpy as jnp
from jax import lax
from jax.sharding import PartitionSpec as P


def project(rows, weight):
    return jnp.dot(rows, weight, preferred_element_type=jnp.float32).astype(jnp.bfloat16)


def project_tangent(tangent, weight):
    count, dirs, width = tangent.shape
    return project(tangent.reshape(count * dirs, width), weight).reshape(count, dirs, width)


def on_device(
    layer_in,
    laplace_in,
    tangent_in,
    spin_labels,
    pair_bias,
    query_weight,
    key_weight,
    value_weight,
    out_weight,
    head_gain,
    spin_gain,
):
    rows, width = layer_in.shape
    heads = head_gain.shape[0]
    head_size = width // heads
    dirs = tangent_in.shape[1]
    scale = 1.0 / math.sqrt(head_size)
    bias_cols = lax.all_to_all(pair_bias, "blk", split_axis=1, concat_axis=0, tiled=True)
    query = project(layer_in, query_weight).reshape(rows, heads, head_size)
    lap_query = project(laplace_in, query_weight).reshape(rows, heads, head_size)
    tan_query = project_tangent(tangent_in, query_weight).reshape(rows, dirs, heads, head_size)
    spin_query = spin_labels.astype(jnp.float32)
    spin_wire = spin_labels.astype(jnp.bfloat16)

    def attend(carry, block, first):
        top, total, numer, tan_total, tan_numer, lap_total, lap_numer, trace_total, trace_numer = (
            carry
        )
        key_b, value_b, lap_key_b, lap_value_b, tan_key_b, tan_value_b, spin_key = block
        count = key_b.shape[0]
        key_h = key_b.reshape(count, heads, head_size)
        value_h = value_b.reshape(count, heads, head_size)
        lap_key_h = lap_key_b.reshape(count, heads, head_size)
        lap_value_h = lap_value_b.reshape(count, heads, head_size)
        tan_key_h = tan_key_b.reshape(count, dirs, heads, head_size)
        tan_value_h = tan_value_b.reshape(count, dirs, heads, head_size)
        bias_rows = lax.dynamic_slice_in_dim(bias_cols, first, count, 0).astype(jnp.float32)
        spin_float = spin_key.astype(jnp.float32)
        same = (
            spin_query[:, None] * spin_float[None, :]
            + (1.0 - spin_query)[:, None] * (1.0 - spin_float)[None, :]
        )
        scores = (
            jnp.einsum("ihd,jhd->hij", query, key_h, preferred_element_type=jnp.float32) * scale
        )
        scores = (
            scores
            + head_gain[:, None, None] * bias_rows.T[None]
            + spin_gain[:, None, None] * same[None]
        )
        new_top = jnp.maximum(top, jnp.max(scores, axis=2))
        shrink = jnp.exp(top - new_top)
        shrink_rows = shrink.T[:, :, None]
        unnorm = jnp.exp(scores - new_top[:, :, None])
        weights = unnorm.astype(jnp.bfloat16)
        total = total * shrink + jnp.sum(unnorm, axis=2)
        numer = numer * shrink_rows + jnp.einsum(
            "hij,jhd->ihd", weights, value_h, preferred_element_type=jnp.float32
        )
        lap_scores = (
            jnp.einsum("ihd,jhd->hij", lap_query, key_h, preferred_element_type=jnp.float32)
            + jnp.einsum("ihd,jhd->hij", query, lap_key_h, preferred_element_type=jnp.float32)
        ) * scale
        lap_weighted = unnorm * lap_scores
        lap_total = lap_total * shrink + jnp.sum(lap_weighted, axis=2)
        lap_numer = (
            lap_numer * shrink_rows
            + jnp.einsum(
                "hij,jhd->ihd",
                lap_weighted.astype(jnp.bfloat16),
                value_h,
                preferred_element_type=jnp.float32,
            )
            + jnp.einsum("hij,jhd->ihd", weights, lap_value_h, preferred_element_type=jnp.float32)
        )
        tan_scores = (
            jnp.einsum("iahd,jhd->ahij", tan_query, key_h, preferred_element_type=jnp.float32)
            + jnp.einsum("ihd,jahd->ahij", query, tan_key_h, preferred_element_type=jnp.float32)
        ) * scale
        cross = (
            jnp.einsum("iahd,jahd->ahij", tan_query, tan_key_h, preferred_element_type=jnp.float32)
            * scale
        )
        tan_weighted = unnorm[None] * tan_scores
        tan_weights = tan_weighted.astype(jnp.bfloat16)
        tan_total = tan_total * shrink[None] + jnp.sum(tan_weighted, axis=3)
        tan_numer = (
            tan_numer * shrink_rows[:, None]
            + jnp.einsum("ahij,jhd->iahd", tan_weights, value_h, preferred_element_type=jnp.float32)
            + jnp.einsum("hij,jahd->iahd", weights, tan_value_h, preferred_element_type=jnp.float32)
        )
        second = unnorm[None] * (tan_scores * tan_scores + 2.0 * cross)
        trace_total = trace_total * shrink + jnp.sum(second, axis=(0, 3))
        trace_numer = (
            trace_numer * shrink_rows
            + jnp.einsum(
                "ahij,jhd->ihd",
                second.astype(jnp.bfloat16),
                value_h,
                preferred_element_type=jnp.float32,
            )
            + 2.0
            * jnp.einsum(
                "ahij,jahd->ihd", tan_weights, tan_value_h, preferred_element_type=jnp.float32
            )
        )
        return (
            new_top,
            total,
            numer,
            tan_total,
            tan_numer,
            lap_total,
            lap_numer,
            trace_total,
            trace_numer,
        )

    head_zeros = jnp.zeros((heads, rows), jnp.float32)
    row_zeros = jnp.zeros((rows, heads, head_size), jnp.float32)
    start_carry = (
        jnp.full((heads, rows), -1e30, jnp.float32),
        head_zeros,
        row_zeros,
        jnp.zeros((dirs, heads, rows), jnp.float32),
        jnp.zeros((rows, dirs, heads, head_size), jnp.float32),
        head_zeros,
        row_zeros,
        head_zeros,
        row_zeros,
    )
    own_keys = project(layer_in, key_weight)
    own_values = project(layer_in, value_weight)
    own_lap_keys = project(laplace_in, key_weight)
    own_lap_values = project(laplace_in, value_weight)
    own_tan_keys = project_tangent(tangent_in, key_weight)
    own_tan_values = project_tangent(tangent_in, value_weight)
    block = (
        lax.all_gather(own_keys, "blk", axis=0, tiled=True),
        lax.all_gather(own_values, "blk", axis=0, tiled=True),
        lax.all_gather(own_lap_keys, "blk", axis=0, tiled=True),
        lax.all_gather(own_lap_values, "blk", axis=0, tiled=True),
        lax.all_gather(own_tan_keys, "blk", axis=0, tiled=True),
        lax.all_gather(own_tan_values, "blk", axis=0, tiled=True),
        lax.all_gather(spin_wire, "blk", axis=0, tiled=True),
    )
    count = block[0].shape[0]
    size = 256
    parts = count // size
    stacked = tuple((piece.reshape((parts, size) + piece.shape[1:]) for piece in block))

    def step(inner, item):
        number, pieces = item
        return (attend(inner, pieces, number * size), None)

    result, _ = lax.scan(step, start_carry, (jnp.arange(parts, dtype=jnp.int32), stacked))
    top, total, numer, tan_total, tan_numer, lap_total, lap_numer, trace_total, trace_numer = result
    denom = total.T[:, :, None]
    denom_sq = denom * denom
    attn = numer / denom
    tan_denom = jnp.transpose(tan_total, (2, 0, 1))[..., None]
    attn_tan = tan_numer / denom[:, None] - numer[:, None] * tan_denom / denom_sq[:, None]
    cross_sum = jnp.sum(tan_numer * tan_denom, axis=1)
    square_sum = jnp.sum(tan_denom * tan_denom, axis=1)
    own_terms = (
        trace_numer / denom
        - numer * trace_total.T[:, :, None] / denom_sq
        - 2.0 * cross_sum / denom_sq
        + 2.0 * numer * square_sum / (denom_sq * denom)
    )
    shared = lax.psum(own_terms.reshape(rows, width).astype(jnp.bfloat16), "tan").astype(
        jnp.float32
    )
    attn_lap = (lap_numer / denom - numer * lap_total.T[:, :, None] / denom_sq).reshape(
        rows, width
    ) + shared
    layer_out = (
        jnp.dot(
            attn.reshape(rows, width).astype(jnp.bfloat16),
            out_weight,
            preferred_element_type=jnp.float32,
        )
        + layer_in.astype(jnp.float32)
    ).astype(jnp.bfloat16)
    tan_flat = attn_tan.reshape(rows * dirs, width).astype(jnp.bfloat16)
    tangent_out = jnp.dot(tan_flat, out_weight, preferred_element_type=jnp.float32).reshape(
        rows, dirs, width
    )
    tangent_out = (tangent_out + tangent_in.astype(jnp.float32)).astype(jnp.bfloat16)
    laplacian_out = jnp.dot(
        attn_lap.astype(jnp.bfloat16), out_weight, preferred_element_type=jnp.float32
    ) + laplace_in.astype(jnp.float32)
    return (layer_out, tangent_out, laplacian_out)


def solution(mesh):
    in_specs = (
        P("blk", None),
        P("blk", None),
        P("blk", "tan", None),
        P("blk"),
        P("blk", None),
        P(),
        P(),
        P(),
        P(),
        P(),
        P(),
    )
    out_specs = (P("blk", None), P("blk", "tan", None), P("blk", None))
    return jax.shard_map(
        on_device, mesh=mesh, in_specs=in_specs, out_specs=out_specs, check_vma=False
    )
```

profile of v0, /device:TPU:8, one launch (start us, length us, event | category | flops | bytes accessed | tf_op | source)
XLA Modules:
  0.0 942.7 jit_solution(8929567075966488008)
XLA Ops:
  7.2 1.8 convolution_convert_fusion.8
  9.1 1.7 convolution_convert_fusion.3
  10.9 1.7 convolution_convert_fusion.6
  12.7 1.7 convolution_convert_fusion.4
  19.4 11.8 %all-to-all-start = ((bf16[128,16,128]{2,0,1:T(8,128)(2,1)}), bf16[128,16,128]{2,0,1:T(8,128)(2,1)}, u32[]{:S(2)}, u32[]{:S(2)}) async-start(bf16[128,16,128]{2,0,1:T(8,128)(2,1)} %copy_bitcast_fusion), calls=%async_computation | async-start | bytes 1048576 | tf_op jit(solution)/shard_map/all_to_all | solution.py:35
  32.5 34.9 %all-gather = bf16[16,1,128]{2,1,0:T(2,128)(2,1)S(1)} all-gather(bf16[1,1,128]{2,1,0:T(2,128)(2,1)S(1)} %get-tuple-element.593), channel_id=1, replica_groups=mesh['blk'=16,'tan'=32] {'blk'}, dimensions={0}, use_global_device_ids=true | all-gather | bytes 4352 | tf_op jit(solution)/shard_map/all_gather | solution.py:162
  69.9 20.5 %all-gather.8.cloned.1.call-done = bf16[2048,256]{1,0:T(8,128)(2,1)} async-done(((bf16[128,256]{1,0:T(8,128)(2,1)}), bf16[2048,256]{1,0:T(8,128)(2,1)}) %all-gather.8.cloned.1.call-update) | async-done | bytes 1048592 | tf_op jit(solution)/shard_map/all_gather | solution.py:156
  90.4 74.6 %all-gather.18.cloned.1.call-done = bf16[2048,256]{1,0:T(8,128)(2,1)} async-done(((bf16[128,256]{1,0:T(8,128)(2,1)}), bf16[2048,256]{1,0:T(8,128)(2,1)}) %all-gather.18.cloned.1.call-update) | async-done | bytes 1048592 | tf_op jit(solution)/shard_map/all_gather | solution.py:159
  165.0 75.4 %all-gather.10.cloned.1.call-done = bf16[2048,256]{1,0:T(8,128)(2,1)} async-done(((bf16[128,256]{1,0:T(8,128)(2,1)}), bf16[2048,256]{1,0:T(8,128)(2,1)}) %all-gather.10.cloned.1.call-update) | async-done | bytes 1048592 | tf_op jit(solution)/shard_map/all_gather | solution.py:157
  240.4 75.2 %all-gather.16.cloned.1.call-done = bf16[2048,256]{1,0:T(8,128)(2,1)} async-done(((bf16[128,256]{1,0:T(8,128)(2,1)}), bf16[2048,256]{1,0:T(8,128)(2,1)}) %all-gather.16.cloned.1.call-update) | async-done | bytes 1048592 | tf_op jit(solution)/shard_map/all_gather | solution.py:158
  315.6 80.3 %all-gather.12.cloned.1.call-done = bf16[2048,2,256]{2,0,1:T(8,128)(2,1)} async-done(((bf16[128,2,256]{2,0,1:T(8,128)(2,1)}), bf16[2048,2,256]{2,0,1:T(8,128)(2,1)}) %all-gather.12.cloned.1.call-update) | async-done | bytes 2097168 | tf_op jit(solution)/shard_map/all_gather | solution.py:160
  395.9 79.9 %all-gather.14.cloned.1.call-done = bf16[2048,2,256]{2,0,1:T(8,128)(2,1)} async-done(((bf16[128,2,256]{2,0,1:T(8,128)(2,1)}), bf16[2048,2,256]{2,0,1:T(8,128)(2,1)}) %all-gather.14.cloned.1.call-update) | async-done | bytes 2097168 | tf_op jit(solution)/shard_map/all_gather | solution.py:161
  476.3 194.2 %while.29 = (s32[]{:T(128)}, f32[4,128]{1,0:T(4,128)S(1)}, f32[4,128]{1,0:T(4,128)}, f32[128,4,64]{0,2,1:T(8,128)}, f32[2,4,128]{2,0,1:T(2,128)S(1)}, /*index=5*...) while((s32[]{:T(128)}, f32[4,128]{1,0:T(4,128)S(1)}, ...), condition=%wide.region_7.8_spmd.clone, body=%wide.region_0.7_spmd.clone.sunk | while | flops 325065856 | bytes 26266780 | solution.py:173
  476.3 1.2 dynamic_slice.87
  479.9 1.6 constant_dynamic-slice_fusion.10
  484.9 1.2 convolution_bitcast_fusion.10
  486.1 1.5 multiply_convert_fusion.2
  488.6 1.4 convert_reduce_fusion.2
  491.5 1.7 fusion.155
  499.9 1.2 dynamic_slice.87
  503.5 1.6 constant_dynamic-slice_fusion.10
  509.7 1.5 multiply_convert_fusion.2
  512.3 1.4 convert_reduce_fusion.2
  513.6 1.2 fusion.146
  515.8 1.8 fusion.155
  524.3 1.2 dynamic_slice.87
  527.9 1.6 constant_dynamic-slice_fusion.10
  534.1 1.5 multiply_convert_fusion.2
  536.6 1.4 convert_reduce_fusion.2
  538.0 1.2 fusion.146
  540.2 1.8 fusion.155
  548.7 1.2 dynamic_slice.87
  552.2 1.6 constant_dynamic-slice_fusion.10
  558.5 1.5 multiply_convert_fusion.2
  561.0 1.4 convert_reduce_fusion.2
  562.4 1.2 fusion.146
  564.6 1.8 fusion.155
  573.1 1.2 dynamic_slice.87
  576.6 1.6 constant_dynamic-slice_fusion.10
  582.8 1.5 multiply_convert_fusion.2
  585.4 1.4 convert_reduce_fusion.2
  586.7 1.2 fusion.146
  589.0 1.8 fusion.155
  597.4 1.2 dynamic_slice.87
  601.0 1.6 constant_dynamic-slice_fusion.10
  607.2 1.5 multiply_convert_fusion.2
  609.7 1.4 convert_reduce_fusion.2
  611.1 1.2 fusion.146
  613.3 1.8 fusion.155
  621.8 1.2 dynamic_slice.87
  625.4 1.6 constant_dynamic-slice_fusion.10
  631.6 1.5 multiply_convert_fusion.2
  634.1 1.4 convert_reduce_fusion.2
  635.5 1.2 fusion.146
  637.7 1.8 fusion.155
  646.2 1.2 dynamic_slice.87
  649.7 1.6 constant_dynamic-slice_fusion.10
  655.9 1.5 multiply_convert_fusion.2
  658.5 1.4 convert_reduce_fusion.2
  659.9 1.2 fusion.146
  662.1 1.8 fusion.155
  672.4 1.8 add_convert_fusion
  674.2 1.2 fusion.36
  677.1 257.1 %all-reduce.2.cloned.1.call-done = bf16[128,256]{0,1:T(8,128)(2,1)} async-done(((bf16[128,256]{0,1:T(8,128)(2,1)}), bf16[128,256]{0,1:T(8,128)(2,1)}) %all-reduce.2.cloned.1.call-update) | async-done | bytes 65552 | tf_op jit(solution)/shard_map/psum | solution.py:188
  (453 shorter events, 131.7 us)
Async XLA Ops:
  7.2 11.3 %copy-start = (bf16[128,2048]{1,0:T(8,128)(2,1)S(1)}, bf16[128,2048]{1,0:T(8,128)(2,1)}, u32[]{:S(2)}) copy-start(bf16[128,2048]{1,0:T(8,128)(2,1)} %param.17) | copy-start | bytes 1572868
  7.2 10.3 %copy-start.5 = (bf16[256,256]{1,0:T(8,128)(2,1)S(1)}, bf16[256,256]{1,0:T(8,128)(2,1)}, u32[]{:S(2)}) copy-start(bf16[256,256]{1,0:T(8,128)(2,1)} %param.20) | copy-start | bytes 393220
  7.2 83.2 %all-gather.8.cloned.1.call-start = ((), (), s32[]{:S(2)}) async-start(), calls=%async_computation.1 | async-start | bytes 1114112 | tf_op jit(solution)/shard_map/all_gather | solution.py:156
  9.1 155.9 %all-gather.18.cloned.1.call-start = ((), (), s32[]{:S(2)}) async-start(), calls=%async_computation.6 | async-start | bytes 1114112 | tf_op jit(solution)/shard_map/all_gather | solution.py:159
  10.9 229.5 %all-gather.10.cloned.1.call-start = ((), (), s32[]{:S(2)}) async-start(), calls=%async_computation.2 | async-start | bytes 1114112 | tf_op jit(solution)/shard_map/all_gather | solution.py:157
  12.7 302.9 %all-gather.16.cloned.1.call-start = ((), (), s32[]{:S(2)}) async-start(), calls=%async_computation.5 | async-start | bytes 1114112 | tf_op jit(solution)/shard_map/all_gather | solution.py:158
  14.5 381.4 %all-gather.12.cloned.1.call-start = ((), (), s32[]{:S(2)}) async-start(), calls=%async_computation.3 | async-start | bytes 2228224 | tf_op jit(solution)/shard_map/all_gather | solution.py:160
  15.5 15.8 %copy-start.6 = (bf16[256,256]{1,0:T(8,128)(2,1)S(1)}, bf16[256,256]{1,0:T(8,128)(2,1)}, u32[]{:S(2)}) copy-start(bf16[256,256]{1,0:T(8,128)(2,1)} %param.18) | copy-start | bytes 393220
  17.4 15.1 %copy-start.18 = (s32[128]{0:T(128)S(1)}, s32[128]{0:T(128)}, u32[]{:S(2)}) copy-start(s32[128]{0:T(128)} %param.16) | copy-start | bytes 1540
  17.4 50.7 %copy-start.8 = (bf16[128,256]{1,0:T(8,128)(2,1)S(1)}, bf16[128,256]{1,0:T(8,128)(2,1)}, u32[]{:S(2)}) copy-start(bf16[128,256]{1,0:T(8,128)(2,1)} %param.13) | copy-start | bytes 196612
  17.4 458.3 %all-gather.14.cloned.1.call-start = ((), (), s32[]{:S(2)}) async-start(), calls=%async_computation.4 | async-start | bytes 2228224 | tf_op jit(solution)/shard_map/all_gather | solution.py:161
  17.8 51.2 %copy-start.10 = (bf16[128,256]{1,0:T(8,128)(2,1)S(1)}, bf16[128,256]{1,0:T(8,128)(2,1)}, u32[]{:S(2)}) copy-start(bf16[128,256]{1,0:T(8,128)(2,1)} %param.14) | copy-start | bytes 196612
  19.4 50.5 %all-to-all-start = ((bf16[128,16,128]{2,0,1:T(8,128)(2,1)}), bf16[128,16,128]{2,0,1:T(8,128)(2,1)}, u32[]{:S(2)}, u32[]{:S(2)}) async-start(bf16[128,16,128]{2,0,1:T(8,128)(2,1)} %copy_bitcast_fusion), calls=%async_computation | async-start | bytes 1048576 | tf_op jit(solution)/shard_map/all_to_all | solution.py:35
  31.2 902.9 %all-reduce.2.cloned.1.call-start = ((), (), s32[]{:S(2)}) async-start(), calls=%async_computation.7 | async-start | bytes 131072 | tf_op jit(solution)/shard_map/psum | solution.py:188
  476.3 5.2 copy-start.16
  490.0 6.7 copy-start.4
  494.4 3.5 copy-start.1
  496.7 2.3 copy-start.2
  497.9 2.1 copy-start.17
  499.9 5.2 copy-start.16
  513.6 7.5 copy-start.4
  518.8 3.5 copy-start.1
  521.1 2.3 copy-start.2
  522.2 1.4 copy-start.14
  522.2 2.1 copy-start.17
  524.3 5.2 copy-start.16
  538.0 7.5 copy-start.4
  543.1 3.5 copy-start.1
  545.5 2.3 copy-start.2
  546.6 1.5 copy-start.14
  546.6 2.1 copy-start.17
  548.7 5.2 copy-start.16
  562.4 7.5 copy-start.4
  567.5 3.5 copy-start.1
  569.8 2.3 copy-start.2
  571.0 1.5 copy-start.14
  571.0 2.1 copy-start.17
  573.1 5.2 copy-start.16
  586.7 7.5 copy-start.4
  591.9 3.5 copy-start.1
  594.2 2.3 copy-start.2
  595.3 1.5 copy-start.14
  595.3 2.1 copy-start.17
  597.4 5.2 copy-start.16
  611.1 7.5 copy-start.4
  616.2 3.5 copy-start.1
  618.6 2.3 copy-start.2
  619.7 1.5 copy-start.14
  619.7 2.1 copy-start.17
  621.8 5.2 copy-start.16
  635.5 7.5 copy-start.4
  640.6 3.5 copy-start.1
  642.9 2.3 copy-start.2
  644.1 1.5 copy-start.14
  644.1 2.1 copy-start.17
  646.2 5.2 copy-start.16
  659.8 7.5 copy-start.4
  665.0 3.5 copy-start.1
  667.3 2.3 copy-start.2
  668.5 1.5 copy-start.14
  668.5 2.1 copy-start.17
  670.5 4.9 copy-start.7
  670.5 4.9 copy-start.9
  670.5 264.5 %copy-start.11 = (bf16[128,256]{1,0:T(8,128)(2,1)S(1)}, bf16[128,256]{1,0:T(8,128)(2,1)}, u32[]{:S(2)}) copy-start(bf16[128,256]{1,0:T(8,128)(2,1)} %param.14) | copy-start | bytes 196612
  (33 other events, 27.7 us)
Sparse Core Ops, SparseCore 0:
  10.7 79.6 all-gather.7
  92.5 72.4 all-gather.17
  167.1 73.2 all-gather.9
  242.3 73.2 all-gather.15
  317.5 78.3 all-gather.11
  397.8 77.8 all-gather.13
  674.3 259.7 all-reduce.1
where the time goes:
time: 947 us; the launch traced here: 943 us
  waiting for transfers between devices  663 us (70%)
  matrix products  112 us (12%)
  local copies, waits for them, and re-layouts  65 us (7%)
  blocking collectives  34.9 us (4%)
  other arithmetic  34.7 us (4%)
  between operations  14.4 us (2%)
  starting transfers between devices  12.1 us (1%)
    psum x1, waiting for transfers between devices, on_device(): lax.psum(own_terms.reshape(rows, width).astype(jnp.bfloat16), 'tan')  257 us
    all_gather x1, waiting for transfers between devices, on_device(): lax.all_gather(own_tan_keys, 'blk', axis=0, tiled=True)  80.3 us
    all_gather x1, waiting for transfers between devices, on_device(): lax.all_gather(own_tan_values, 'blk', axis=0, tiled=True)  79.9 us
    all_gather x1, waiting for transfers between devices, on_device(): lax.all_gather(own_values, 'blk', axis=0, tiled=True)  75.4 us
    all_gather x1, waiting for transfers between devices, on_device(): lax.all_gather(own_lap_keys, 'blk', axis=0, tiled=True)  75.2 us
    all_gather x1, waiting for transfers between devices, on_device(): lax.all_gather(own_lap_values, 'blk', axis=0, tiled=True)  74.6 us
    dynamic_slice x80, local copies, waits for them, and re-layouts, on_device(): lax.scan(step, start_carry, (jnp.arange(parts, dtype=jnp.int32), stacked))  52.4 us
    all_gather x1, blocking collectives, on_device(): lax.all_gather(spin_wire, 'blk', axis=0, tiled=True)  34.9 us
  transfers between devices with their start and end apart: 8, of which 7 were waited for; matrix products, arithmetic and copies ran while one was open for 2% of the time, Pallas kernels for 0%

commit v1 on v0

--- a/solution.py
+++ b/solution.py
@@ -3,6 +3,13 @@
 import jax.numpy as jnp
 from jax import lax
 from jax.sharding import PartitionSpec as P
+
+
+def all_by_exchange(value, name, dim):
+    size = lax.axis_size(name)
+    blocks = jnp.stack([value for _ in range(size)])
+    blocks = lax.all_to_all(blocks, name, split_axis=0, concat_axis=0)
+    return jnp.concatenate(blocks, axis=dim)
 
 
 def project(rows, weight):
@@ -157,7 +164,7 @@
         lax.all_gather(own_values, "blk", axis=0, tiled=True),
         lax.all_gather(own_lap_keys, "blk", axis=0, tiled=True),
         lax.all_gather(own_lap_values, "blk", axis=0, tiled=True),
-        lax.all_gather(own_tan_keys, "blk", axis=0, tiled=True),
+        all_by_exchange(own_tan_keys, "blk", 0),
         lax.all_gather(own_tan_values, "blk", axis=0, tiled=True),
         lax.all_gather(spin_wire, "blk", axis=0, tiled=True),
     )

time: 947 us -> 867 us (0.916)
  waiting for transfers between devices: 663 us -> 586 us
    all_gather x1 -> x0, waiting for transfers between devices: 80.3 us -> none  [on_device(): lax.all_gather(own_tan_keys, 'blk', axis=0, tiled=True)]
    all_to_all x0 -> x1, waiting for transfers between devices: none -> 53.8 us  [all_by_exchange(): blocks = lax.all_to_all(blocks, name, split_axis=0, concat_axis=0)]
    all_gather x1, waiting for transfers between devices: 74.6 us -> 43.9 us  [on_device(): lax.all_gather(own_lap_values, 'blk', axis=0, tiled=True)]
    all_gather x1, waiting for transfers between devices: 20.5 us -> 0.01 us  [on_device(): lax.all_gather(own_keys, 'blk', axis=0, tiled=True)]
    all_to_all x0 -> x1, starting transfers between devices: none -> 11.9 us  [all_by_exchange(): blocks = lax.all_to_all(blocks, name, split_axis=0, concat_axis=0)]
  transfers between devices with their start and end apart: 8 -> 8, of which waited for: 7 -> 6; matrix products, arithmetic and copies ran while one was open for 2% -> 2% of each run, Pallas kernels for 0% -> 0%
where the time goes in v1:
time: 867 us; the launch traced here: 863 us
  waiting for transfers between devices  586 us (68%)
  matrix products  111 us (13%)
  local copies, waits for them, and re-layouts  61.3 us (7%)
  blocking collectives  32.7 us (4%)
  other arithmetic  30 us (3%)
  starting transfers between devices  19.8 us (2%)
  between operations  14.4 us (2%)
    psum x1, waiting for transfers between devices, on_device(): lax.psum(own_terms.reshape(rows, width).astype(jnp.bfloat16), 'tan')  257 us
    all_gather x1, waiting for transfers between devices, on_device(): lax.all_gather(own_tan_values, 'blk', axis=0, tiled=True)  80.3 us
    all_gather x1, waiting for transfers between devices, on_device(): lax.all_gather(own_lap_keys, 'blk', axis=0, tiled=True)  75.2 us
    all_gather x1, waiting for transfers between devices, on_device(): lax.all_gather(own_values, 'blk', axis=0, tiled=True)  75.2 us
    all_to_all x1, waiting for transfers between devices, all_by_exchange(): blocks = lax.all_to_all(blocks, name, split_axis=0, concat_axis=0)  53.8 us
    dynamic_slice x80, local copies, waits for them, and re-layouts, on_device(): lax.scan(step, start_carry, (jnp.arange(parts, dtype=jnp.int32), stacked))  47.3 us
    all_gather x1, waiting for transfers between devices, on_device(): lax.all_gather(own_lap_values, 'blk', axis=0, tiled=True)  43.9 us
    all_gather x1, blocking collectives, on_device(): lax.all_gather(spin_wire, 'blk', axis=0, tiled=True)  32.7 us
  transfers between devices with their start and end apart: 8, of which 6 were waited for; matrix products, arithmetic and copies ran while one was open for 2% of the time, Pallas kernels for 0%

profile of v1, /device:TPU:8, one launch (start us, length us, event | category | flops | bytes accessed | tf_op | source)
XLA Modules:
  0.0 863.1 jit_solution(13705068613016763588)
XLA Ops:
  7.2 1.8 convolution_convert_fusion.8
  9.1 1.7 convolution_convert_fusion.3
  10.9 1.7 convolution_convert_fusion.6
  12.7 1.7 convolution_convert_fusion.4
  16.6 1.6 stack.3
  18.2 11.9 %all-to-all-start.1 = ((bf16[16,128,2,256]{3,1,2,0:T(8,128)(2,1)}), bf16[16,128,2,256]{3,1,2,0:T(8,128)(2,1)S(1)}, u32[]{:S(2)}, u32[]{:S(2)}) async-start(bf16[16,128,2,256]{3,1,2,0:T(8,128)(2,1)} %stack.3), calls=%async_computation.1 | async-start | bytes 4194304 | tf_op jit(solution)/shard_map/all_to_all | solution.py:11
  32.1 53.8 %all-to-all-done.1 = bf16[16,128,2,256]{3,1,2,0:T(8,128)(2,1)S(1)} async-done(((bf16[16,128,2,256]{3,1,2,0:T(8,128)(2,1)}), bf16[16,128,2,256]{3,1,2,0:T(8,128)(2,1)S(1)}, u32[]{:S(2)}, u32[]{:S(2)}) %all-to-all-start.1) | async-done | bytes 2097184 | tf_op jit(solution)/shard_map/all_to_all | solution.py:11
  85.9 7.6 all-to-all-start
  94.8 32.7 %all-gather = bf16[16,1,128]{2,1,0:T(2,128)(2,1)S(1)} all-gather(bf16[1,1,128]{2,1,0:T(2,128)(2,1)S(1)} %get-tuple-element.593), channel_id=1, replica_groups=mesh['blk'=16,'tan'=32] {'blk'}, dimensions={0}, use_global_device_ids=true | all-gather | bytes 4352 | tf_op jit(solution)/shard_map/all_gather | solution.py:169
  129.4 1.5 copy.99
  130.8 43.9 %all-gather.15.cloned.1.call-done = bf16[2048,256]{1,0:T(8,128)(2,1)} async-done(((bf16[128,256]{1,0:T(8,128)(2,1)}), bf16[2048,256]{1,0:T(8,128)(2,1)}) %all-gather.15.cloned.1.call-update) | async-done | bytes 1048592 | tf_op jit(solution)/shard_map/all_gather | solution.py:166
  174.7 75.2 %all-gather.9.cloned.1.call-done = bf16[2048,256]{1,0:T(8,128)(2,1)} async-done(((bf16[128,256]{1,0:T(8,128)(2,1)}), bf16[2048,256]{1,0:T(8,128)(2,1)}) %all-gather.9.cloned.1.call-update) | async-done | bytes 1048592 | tf_op jit(solution)/shard_map/all_gather | solution.py:164
  249.9 75.2 %all-gather.13.cloned.1.call-done = bf16[2048,256]{1,0:T(8,128)(2,1)} async-done(((bf16[128,256]{1,0:T(8,128)(2,1)}), bf16[2048,256]{1,0:T(8,128)(2,1)}) %all-gather.13.cloned.1.call-update) | async-done | bytes 1048592 | tf_op jit(solution)/shard_map/all_gather | solution.py:165
  325.1 80.3 %all-gather.11.cloned.1.call-done = bf16[2048,2,256]{2,0,1:T(8,128)(2,1)} async-done(((bf16[128,2,256]{2,0,1:T(8,128)(2,1)}), bf16[2048,2,256]{2,0,1:T(8,128)(2,1)}) %all-gather.11.cloned.1.call-update) | async-done | bytes 2097168 | tf_op jit(solution)/shard_map/all_gather | solution.py:168
  405.5 185.5 %while.29 = (s32[]{:T(128)}, f32[4,128]{1,0:T(4,128)S(1)}, f32[4,128]{1,0:T(4,128)}, f32[128,4,64]{0,2,1:T(8,128)}, f32[2,4,128]{2,0,1:T(2,128)S(1)}, /*index=5*...) while((s32[]{:T(128)}, f32[4,128]{1,0:T(4,128)S(1)}, ...), condition=%wide.region_7.8_spmd.clone, body=%wide.region_0.7_spmd.clone.sunk | while | flops 325065856 | bytes 26300116 | solution.py:180
  407.8 1.6 constant_dynamic-slice_fusion.10
  412.8 1.2 convolution_bitcast_fusion.10
  414.0 1.5 multiply_convert_fusion.2
  416.5 1.4 convert_reduce_fusion.2
  419.5 1.7 fusion.155
  430.3 1.6 constant_dynamic-slice_fusion.10
  435.3 1.2 convolution_bitcast_fusion.10
  436.5 1.5 multiply_convert_fusion.2
  439.0 1.4 convert_reduce_fusion.2
  440.4 1.3 fusion.146
  442.7 1.8 fusion.155
  453.6 1.6 constant_dynamic-slice_fusion.10
  458.6 1.2 convolution_bitcast_fusion.10
  459.7 1.5 multiply_convert_fusion.2
  462.3 1.4 convert_reduce_fusion.2
  463.7 1.3 fusion.146
  466.0 1.8 fusion.155
  476.8 1.6 constant_dynamic-slice_fusion.10
  481.8 1.2 convolution_bitcast_fusion.10
  483.0 1.5 multiply_convert_fusion.2
  485.6 1.4 convert_reduce_fusion.2
  487.0 1.3 fusion.146
  489.3 1.8 fusion.155
  500.1 1.6 constant_dynamic-slice_fusion.10
  505.1 1.2 convolution_bitcast_fusion.10
  506.3 1.5 multiply_convert_fusion.2
  508.9 1.4 convert_reduce_fusion.2
  510.2 1.3 fusion.146
  512.6 1.8 fusion.155
  523.4 1.6 constant_dynamic-slice_fusion.10
  528.4 1.2 convolution_bitcast_fusion.10
  529.6 1.5 multiply_convert_fusion.2
  532.1 1.4 convert_reduce_fusion.2
  533.5 1.3 fusion.146
  535.9 1.8 fusion.155
  546.7 1.6 constant_dynamic-slice_fusion.10
  551.7 1.2 convolution_bitcast_fusion.10
  552.9 1.5 multiply_convert_fusion.2
  555.4 1.4 convert_reduce_fusion.2
  556.8 1.3 fusion.146
  559.1 1.8 fusion.155
  570.0 1.6 constant_dynamic-slice_fusion.10
  576.2 1.5 multiply_convert_fusion.2
  578.7 1.4 convert_reduce_fusion.2
  580.1 1.3 fusion.146
  582.4 1.8 fusion.155
  592.9 1.8 add_convert_fusion
  594.6 1.2 fusion.36
  597.5 257.0 %all-reduce.2.cloned.1.call-done = bf16[128,256]{0,1:T(8,128)(2,1)} async-done(((bf16[128,256]{0,1:T(8,128)(2,1)}), bf16[128,256]{0,1:T(8,128)(2,1)}) %all-reduce.2.cloned.1.call-update) | async-done | bytes 65552 | tf_op jit(solution)/shard_map/psum | solution.py:195
  (554 shorter events, 122.0 us)
Async XLA Ops:
  7.2 24.0 %copy-start = (bf16[128,2048]{1,0:T(8,128)(2,1)S(1)}, bf16[128,2048]{1,0:T(8,128)(2,1)}, u32[]{:S(2)}) copy-start(bf16[128,2048]{1,0:T(8,128)(2,1)} %param.17) | copy-start | bytes 1572868
  7.2 123.7 %all-gather.7.cloned.1.call-start = ((), (), s32[]{:S(2)}) async-start(), calls=%async_computation.2 | async-start | bytes 1114112 | tf_op jit(solution)/shard_map/all_gather | solution.py:163
  9.0 165.7 %all-gather.15.cloned.1.call-start = ((), (), s32[]{:S(2)}) async-start(), calls=%async_computation.6 | async-start | bytes 1114112 | tf_op jit(solution)/shard_map/all_gather | solution.py:166
  10.8 239.1 %all-gather.9.cloned.1.call-start = ((), (), s32[]{:S(2)}) async-start(), calls=%async_computation.3 | async-start | bytes 1114112 | tf_op jit(solution)/shard_map/all_gather | solution.py:164
  12.6 312.5 %all-gather.13.cloned.1.call-start = ((), (), s32[]{:S(2)}) async-start(), calls=%async_computation.5 | async-start | bytes 1114112 | tf_op jit(solution)/shard_map/all_gather | solution.py:165
  18.2 12.0 %copy-start.5 = (bf16[256,256]{1,0:T(8,128)(2,1)S(1)}, bf16[256,256]{1,0:T(8,128)(2,1)}, u32[]{:S(2)}) copy-start(bf16[256,256]{1,0:T(8,128)(2,1)} %param.20) | copy-start | bytes 393220
  18.2 67.7 %all-to-all-start.1 = ((bf16[16,128,2,256]{3,1,2,0:T(8,128)(2,1)}), bf16[16,128,2,256]{3,1,2,0:T(8,128)(2,1)S(1)}, u32[]{:S(2)}, u32[]{:S(2)}) async-start(bf16[16,128,2,256]{3,1,2,0:T(8,128)(2,1)} %stack.3), calls=%async_computation.1 | async-start | bytes 4194304 | tf_op jit(solution)/shard_map/all_to_all | solution.py:11
  30.1 63.5 %copy-start.6 = (bf16[256,256]{1,0:T(8,128)(2,1)S(1)}, bf16[256,256]{1,0:T(8,128)(2,1)}, u32[]{:S(2)}) copy-start(bf16[256,256]{1,0:T(8,128)(2,1)} %param.18) | copy-start | bytes 393220
  30.1 64.7 %copy-start.24 = (s32[128]{0:T(128)S(1)}, s32[128]{0:T(128)}, u32[]{:S(2)}) copy-start(s32[128]{0:T(128)} %param.16) | copy-start | bytes 1540
  30.1 97.5 %copy-start.8 = (bf16[128,256]{1,0:T(8,128)(2,1)S(1)}, bf16[128,256]{1,0:T(8,128)(2,1)}, u32[]{:S(2)}) copy-start(bf16[128,256]{1,0:T(8,128)(2,1)} %param.13) | copy-start | bytes 196612
  30.1 375.3 %all-gather.11.cloned.1.call-start = ((), (), s32[]{:S(2)}) async-start(), calls=%async_computation.4 | async-start | bytes 2228224 | tf_op jit(solution)/shard_map/all_gather | solution.py:168
  30.4 98.0 %copy-start.10 = (bf16[128,256]{1,0:T(8,128)(2,1)S(1)}, bf16[128,256]{1,0:T(8,128)(2,1)}, u32[]{:S(2)}) copy-start(bf16[128,256]{1,0:T(8,128)(2,1)} %param.14) | copy-start | bytes 196612
  85.9 44.9 %all-to-all-start = ((bf16[128,16,128]{2,0,1:T(8,128)(2,1)}), bf16[128,16,128]{2,0,1:T(8,128)(2,1)}, u32[]{:S(2)}, u32[]{:S(2)}) async-start(bf16[128,16,128]{2,0,1:T(8,128)(2,1)} %copy_bitcast_fusion), calls=%async_computation | async-start | bytes 1048576 | tf_op jit(solution)/shard_map/all_to_all | solution.py:42
  93.5 761.0 %all-reduce.2.cloned.1.call-start = ((), (), s32[]{:S(2)}) async-start(), calls=%async_computation.7 | async-start | bytes 131072 | tf_op jit(solution)/shard_map/psum | solution.py:195
  129.4 276.1 %copy-start.18 = (f32[4]{0:T(128)S(1)}, f32[4]{0:T(128)}, u32[]{:S(2)}) copy-start(f32[4]{0:T(128)} %param.22) | copy-start | bytes 52
  129.4 276.1 %copy-start.20 = (f32[4]{0:T(128)S(1)}, f32[4]{0:T(128)}, u32[]{:S(2)}) copy-start(f32[4]{0:T(128)} %param.23) | copy-start | bytes 52
  405.5 7.1 copy-start.16
  405.5 7.1 copy-start.22
  417.9 6.8 copy-start.4
  422.4 3.5 copy-start.1
  424.7 2.4 copy-start.2
  428.0 2.2 copy-start.25
  428.0 7.1 copy-start.16
  428.0 7.1 copy-start.22
  440.4 7.6 copy-start.4
  445.6 3.5 copy-start.1
  448.0 2.4 copy-start.2
  451.2 2.2 copy-start.25
  451.3 7.1 copy-start.16
  451.3 7.1 copy-start.22
  463.7 7.6 copy-start.4
  468.9 3.5 copy-start.1
  471.2 2.4 copy-start.2
  474.5 2.2 copy-start.25
  474.5 7.1 copy-start.16
  474.6 7.1 copy-start.22
  486.9 7.6 copy-start.4
  492.2 3.5 copy-start.1
  494.5 2.4 copy-start.2
  497.8 2.2 copy-start.25
  497.8 7.1 copy-start.16
  497.8 7.1 copy-start.22
  510.2 7.6 copy-start.4
  515.5 3.5 copy-start.1
  517.8 2.4 copy-start.2
  521.1 7.1 copy-start.16
  521.1 7.1 copy-start.22
  533.5 7.6 copy-start.4
  538.8 3.5 copy-start.1
  541.1 2.4 copy-start.2
  544.4 2.2 copy-start.25
  544.4 7.1 copy-start.16
  544.4 7.1 copy-start.22
  556.8 7.6 copy-start.4
  562.1 3.5 copy-start.1
  564.4 2.4 copy-start.2
  567.7 7.1 copy-start.16
  567.7 7.1 copy-start.22
  580.1 7.6 copy-start.4
  585.3 3.5 copy-start.1
  587.7 2.4 copy-start.2
  590.9 4.9 copy-start.7
  591.0 4.9 copy-start.9
  591.0 264.4 %copy-start.11 = (bf16[128,256]{1,0:T(8,128)(2,1)S(1)}, bf16[128,256]{1,0:T(8,128)(2,1)}, u32[]{:S(2)}) copy-start(bf16[128,256]{1,0:T(8,128)(2,1)} %param.14) | copy-start | bytes 196612
  (83 other events, 128.5 us)
Sparse Core Ops, SparseCore 0:
  10.6 89.0 all-gather.6
  101.8 72.8 all-gather.14
  176.8 73.0 all-gather.8
  251.8 73.2 all-gather.12
  327.0 78.3 all-gather.10
  594.8 259.7 all-reduce.1
